TPU v7x, 512 devices: a whole 4x8x8 slice. The times are simulated.
512 devices in a mesh: expert: 128 (over y, z, core), dp: 4 (over x).
Axes of the slice: x: 4, y: 8, z: 8, core: 2. Of those that a mesh axis runs over, the one named last changes fastest.
Arguments:
- hidden: bfloat16 [128, 4, 256, 1024], P('expert', 'dp'), may hold values from -6 to 6
- w_down: bfloat16 [128, 1024, 3584], P('expert', 'dp'), may hold values from -0.1875 to 0.1875
- expert_ids: int32 [4, 2048, 8], P('dp', 'expert'), may hold values from 0 to 127, all different within a row; in each aligned block of 16 rows (0 to 15, 16 to 31, ..., all dimensions but the last counted through in order) at most 2 rows name the same one
- route_weights: float32 [4, 2048, 8], P('dp', 'expert'), may hold values from 0.1 to 0.6
- grad_out: bfloat16 [4, 2048, 3584], P('dp', 'expert'), may hold values from -6 to 6
Outputs:
- mixed: bfloat16 [4, 2048, 3584], P('dp', 'expert')
- d_hidden: bfloat16 [128, 4, 256, 1024], P('expert', 'dp')
- d_w_down: bfloat16 [128, 1024, 3584], P('expert', 'dp')
- d_route: float32 [4, 2048, 8], P('dp', 'expert')
Inputs may be any that keep to these rules, and one draw needn't show every extreme that they name: `expert_ids`: among the 16 tokens of one device no expert is chosen more than 2 times, and some expert is chosen exactly 2 times; the 8 choices of a token are distinct.
All inputs are finite; a program needn't handle non-finite values.
Results may differ from a plain program's by a relative error of at most 0.0085.
Values may be sent and summed in bfloat16 or wider, within the bound.
A program may use at most 128 MiB of HBM per device.

v0:
```python
import jax
import jax.numpy as jnp
from jax import lax
from jax.sharding import PartitionSpec as P
from jax.experimental.layout import Layout, with_layout_constraint


def slot_ranks(choices, experts):
    flat = choices.reshape(-1)
    onehot = (flat[:, None] == jnp.arange(experts, dtype=jnp.int32)[None, :]).astype(jnp.int32)
    earlier = jnp.cumsum(onehot, axis=0) - onehot
    return jnp.sum(earlier * onehot, axis=1).reshape(choices.shape)


def on_device(hidden, w_down, expert_ids, route_weights, grad_out):
    experts = lax.axis_size("expert")
    groups = lax.axis_size("dp")
    slots = hidden.shape[2] // experts
    width = w_down.shape[2]
    w_whole = lax.all_gather(w_down, "dp", axis=1, tiled=True)[0]
    out_slots = jnp.dot(hidden[0, 0], w_whole, preferred_element_type=jnp.float32).astype(
        jnp.bfloat16
    )
    arrived = lax.all_to_all(
        out_slots.reshape(experts, slots, width), "expert", split_axis=0, concat_axis=0, tiled=True
    )
    arrived = arrived.reshape(experts * slots, width)
    choices = expert_ids[0]
    weights = route_weights[0]
    cotangent = grad_out[0].astype(jnp.float32)
    rows = choices * slots + slot_ranks(choices, experts)
    out_pair = arrived[rows].astype(jnp.float32)
    mixed = jnp.einsum("tk,tkd->td", weights, out_pair)
    d_route = jnp.einsum("td,tkd->tk", cotangent, out_pair)
    grad_pair = (weights[..., None] * cotangent[:, None, :]).astype(jnp.bfloat16)
    outgoing = jnp.zeros((experts * slots, width), jnp.bfloat16)
    outgoing = outgoing.at[rows.reshape(-1)].set(grad_pair.reshape(-1, width))
    mine = lax.all_to_all(
        outgoing.reshape(experts, 1, slots, width),
        "expert",
        split_axis=0,
        concat_axis=0,
        tiled=True,
    )
    own_grads = mine[:, 0]
    slot_grads = lax.all_gather(mine, "dp", axis=1, tiled=True)
    slot_grads = with_layout_constraint(slot_grads, Layout(major_to_minor=(1, 0, 2, 3)))
    d_hidden = jnp.einsum(
        "rd,hd->rh", own_grads.reshape(-1, width), w_whole, preferred_element_type=jnp.float32
    ).astype(jnp.bfloat16)
    columns = lax.all_to_all(hidden, "dp", split_axis=3, concat_axis=1, tiled=True)[0]
    columns = columns.reshape(groups, experts, slots, columns.shape[-1])
    d_weight = jnp.einsum(
        "gsch,sgcd->hd", columns, slot_grads, preferred_element_type=jnp.float32
    ).astype(jnp.bfloat16)
    d_weight = with_layout_constraint(d_weight, Layout(major_to_minor=(0, 1)))
    return (
        mixed.astype(jnp.bfloat16)[None],
        d_hidden.reshape(hidden.shape),
        d_weight[None],
        d_route[None],
    )


def solution(mesh):
    placed = (
        P("expert", "dp", None, None),
        P("expert", "dp", None),
        P("dp", "expert", None),
        P("dp", "expert", None),
        P("dp", "expert", None),
    )
    return jax.shard_map(
        on_device,
        mesh=mesh,
        in_specs=placed,
        out_specs=(
            P("dp", "expert", None),
            P("expert", "dp", None, None),
            P("expert", "dp", None),
            P("dp", "expert", None),
        ),
        check_vma=False,
    )
```

profile of v0, /device:TPU:1, one launch (start us, length us, event | category | flops | bytes accessed | tf_op | source)
XLA Modules:
  0.0 196.7 jit_solution(17713640946967735479)
XLA Ops:
  7.2 0.7 all-gather.3.cloned.1.call-update
  9.0 2.5 %scatter_custom_fusion = bf16[256,3584]{1,0:T(8,128)(2,1)S(1)} fusion(s32[128]{0:T(128)S(1)} %fusion.39, f32[16,3584]{1,0:T(8,128)S(1)} %bitcast_convert_fusion.1, f32[128]{0:T(128)S(1)} %mul.53, bf16[]{:T(256)} %constant.7.clone.1), kind=kCustom, calls=%fused_computation.16 | custom fusion | flops 917504 | bytes 2064898 | tf_op jit(solution)/shard_map/scatter | solution.py:37
  11.5 1.6 reshape.99
  13.2 64.9 %all_to_all.25 = bf16[128,1,2,3584]{3,2,1,0:T(2,128)(2,1)S(1)} all-to-all(bf16[128,1,2,3584]{3,2,1,0:T(2,128)(2,1)} %reshape.99), channel_id=1, replica_groups=mesh['expert'=128,'dp'=4] {'expert'}, dimensions={0} | all-to-all | bytes 3670016 | tf_op jit(solution)/shard_map/all_to_all | solution.py:38
  78.1 1.4 copy.38
  79.5 1.0 copy-done
  80.5 0.8 copy.40
  81.9 3.8 %reduce = bf16[1024,256]{1,0:T(8,128)(2,1)S(1)} reduce(bf16[1024,1,1,256]{3,2,1,0:T(2,128)(2,1)S(1)} %bitcast.74, bf16[]{:T(256)} %broadcast.58), dimensions={1,2}, to_apply=%bitcast.67.reduce_sub_computation | reduce | bytes 1048578
  85.7 0.9 reshape.125
  86.6 4.0 %all-to-all-start.2 = ((bf16[4,2,32768]{2,1,0:T(2,128)(2,1)}), bf16[4,2,32768]{2,1,0:T(2,128)(2,1)S(1)}, u32[]{:S(2)}, u32[]{:S(2)}) async-start(bf16[4,2,32768]{2,1,0:T(2,128)(2,1)} %reshape.125), calls=%async_computation.2 | async-start | bytes 1048576 | tf_op jit(solution)/shard_map/all_to_all | solution.py:51
  90.7 4.8 %all-gather.3.cloned.1.call-done = bf16[1,1024,3584]{2,1,0:T(8,128)(2,1)} async-done(((bf16[1,256,3584]{2,1,0:T(8,128)(2,1)}), bf16[1,1024,3584]{2,1,0:T(8,128)(2,1)}) %all-gather.3.cloned.1.call-update) | async-done | bytes 7340048 | tf_op jit(solution)/shard_map/all_gather | solution.py:20
  95.5 6.4 %fusion.12 = bf16[256,3584]{1,0:T(8,128)(2,1)} fusion(bf16[1,1024,3584]{2,1,0:T(8,128)(2,1)} %all-gather.3.cloned.1.call-done, bf16[1,1,256,1024]{3,2,1,0:T(8,128)(2,1)S(1)} %copy-done.1), kind=kOutput, calls=%fused_computation.10 | convolution fusion | flops 1879965696 | bytes 9699328 | tf_op jit(solution)/shard_map/dot_general | solution.py:21
  101.9 4.7 %reshape.96 = bf16[128,2,3584]{2,1,0:T(2,128)(2,1)} reshape(bf16[256,3584]{1,0:T(8,128)(2,1)} %fusion.12) | data formatting | bytes 3670016 | tf_op jit(solution)/shard_map/reshape | solution.py:25
  106.6 20.3 %all-to-all-start = ((bf16[128,2,3584]{2,1,0:T(2,128)(2,1)}), bf16[128,2,3584]{2,1,0:T(2,128)(2,1)}, u32[]{:S(2)}, u32[]{:S(2)}) async-start(bf16[128,2,3584]{2,1,0:T(2,128)(2,1)} %reshape.96), calls=%async_computation | async-start | bytes 3670016 | tf_op jit(solution)/shard_map/all_to_all | solution.py:24
  128.3 1.6 reshape_squeeze.6
  129.9 6.6 %fusion.22 = bf16[1,1,256,1024]{3,2,1,0:T(8,128)(2,1)} fusion(bf16[256,3584]{1,0:T(8,128)(2,1)} %reshape_squeeze.6, bf16[1,1024,3584]{2,1,0:T(8,128)(2,1)} %all-gather.3.cloned.1.call-done), kind=kOutput, calls=%fused_computation.15 | convolution fusion | flops 1879310336 | bytes 9699328 | tf_op jit(solution)/shard_map/rd,hd->rh/dot_general | solution.py:48
  136.6 36.5 %all-to-all-done = bf16[128,2,3584]{2,1,0:T(2,128)(2,1)} async-done(((bf16[128,2,3584]{2,1,0:T(2,128)(2,1)}), bf16[128,2,3584]{2,1,0:T(2,128)(2,1)}, u32[]{:S(2)}, u32[]{:S(2)}) %all-to-all-start) | async-done | bytes 1835040 | tf_op jit(solution)/shard_map/all_to_all | solution.py:24
  173.1 4.1 %reshape.97 = bf16[256,3584]{1,0:T(8,128)(2,1)S(1)} reshape(bf16[128,2,3584]{2,1,0:T(2,128)(2,1)} %all-to-all-done) | data formatting | bytes 3670016 | tf_op jit(solution)/shard_map/reshape | solution.py:27
  177.2 1.1 gather_fusion
  178.7 0.7 copy.66
  179.3 0.6 fusion.29
  179.9 0.7 copy.48
  180.6 2.8 %all-gather.5.cloned.1.call-done = bf16[128,4,2,3584]{3,0,2,1:T(8,128)(2,1)} async-done(((bf16[128,1,2,3584]{3,0,2,1:T(8,128)(2,1)}), bf16[128,4,2,3584]{3,0,2,1:T(8,128)(2,1)}) %all-gather.5.cloned.1.call-update) | async-done | bytes 7340048 | tf_op jit(solution)/shard_map/all_gather | solution.py:46
  183.4 6.4 %fusion.15 = bf16[1,256,3584]{2,1,0:T(8,128)(2,1)} fusion(bf16[128,4,2,3584]{3,0,2,1:T(8,128)(2,1)} %all-gather.5.cloned.1.call-done, bf16[4,128,2,256]{3,0,2,1:T(4,128)(2,1)S(1)} %bitcast.76), kind=kOutput, calls=%fused_computation.11 | convolution fusion | flops 1879965696 | bytes 9699328 | tf_op jit(solution)/shard_map/gsch,sgcd->hd/dot_general | solution.py:53
  (37 shorter events, 3.3 us)
Async XLA Ops:
  7.2 0.8 copy-start.3
  7.2 1.1 copy-start.4
  7.2 1.8 copy-start.2
  7.2 88.3 %all-gather.3.cloned.1.call-start = ((), (), s32[]{:S(2)}) async-start(), calls=%async_computation.3 | async-start | bytes 9175040 | tf_op jit(solution)/shard_map/all_gather | solution.py:20
  7.9 175.5 %all-gather.5.cloned.1.call-start = ((), (), s32[]{:S(2)}) async-start(), calls=%async_computation.4 | async-start | bytes 9175040 | tf_op jit(solution)/shard_map/all_gather | solution.py:46
  79.5 1.0 copy-start
  85.7 9.8 %copy-start.1 = (bf16[1,1,256,1024]{3,2,1,0:T(8,128)(2,1)S(1)}, bf16[1,1,256,1024]{3,2,1,0:T(8,128)(2,1)}, u32[]{:S(2)}) copy-start(bf16[1,1,256,1024]{3,2,1,0:T(8,128)(2,1)} %param.5) | copy-start | bytes 1572868
  86.6 20.0 %all-to-all-start.2 = ((bf16[4,2,32768]{2,1,0:T(2,128)(2,1)}), bf16[4,2,32768]{2,1,0:T(2,128)(2,1)S(1)}, u32[]{:S(2)}, u32[]{:S(2)}) async-start(bf16[4,2,32768]{2,1,0:T(2,128)(2,1)} %reshape.125), calls=%async_computation.2 | async-start | bytes 1048576 | tf_op jit(solution)/shard_map/all_to_all | solution.py:51
  106.6 66.5 %all-to-all-start = ((bf16[128,2,3584]{2,1,0:T(2,128)(2,1)}), bf16[128,2,3584]{2,1,0:T(2,128)(2,1)}, u32[]{:S(2)}, u32[]{:S(2)}) async-start(bf16[128,2,3584]{2,1,0:T(2,128)(2,1)} %reshape.96), calls=%async_computation | async-start | bytes 3670016 | tf_op jit(solution)/shard_map/all_to_all | solution.py:24
Sparse Core Ops, SparseCore 0:
  10.1 85.3 all-gather.2
  97.6 85.7 all-gather.4
where the time goes:
time: 197 us
  blocking collectives  64.9 us (33%)
  waiting for transfers between devices  44.9 us (23%)
  starting transfers between devices  24.4 us (12%)
  local copies, waits for them, and re-layouts  21.1 us (11%)
  matrix products  20.4 us (10%)
  between operations  14.2 us (7%)
  other arithmetic  6.83 us (3%)
    all_to_all x1, blocking collectives, on_device(): lax.all_to_all(outgoing.reshape(experts, 1, slots, width), 'expert', spli...  64.9 us
    all_to_all x1, waiting for transfers between devices, on_device(): lax.all_to_all(out_slots.reshape(experts, slots, width), 'expert', split_...  36.5 us
    all_to_all x1, starting transfers between devices, on_device(): lax.all_to_all(out_slots.reshape(experts, slots, width), 'expert', split_...  20.3 us
    dot_general x1, matrix products, on_device(): jnp.einsum('rd,hd->rh', own_grads.reshape(-1, width), w_whole, preferred_...  6.64 us
    dot_general x1, matrix products, on_device(): jnp.einsum('gsch,sgcd->hd', columns, slot_grads, preferred_element_type=j...  6.41 us
    dot_general x1, matrix products, on_device(): jnp.dot(hidden[0, 0], w_whole, preferred_element_type=jnp.float32)  6.37 us
    all_gather x1, waiting for transfers between devices, on_device(): w_whole = lax.all_gather(w_down, 'dp', axis=1, tiled=True)[0]  4.83 us
    reshape x1, local copies, waits for them, and re-layouts, on_device(): out_slots.reshape(experts, slots, width)  4.75 us
  transfers between devices with their start and end apart: 4, of which 3 were waited for; matrix products, arithmetic and copies ran while one was open for 21% of the time, Pallas kernels for 0%

commit v1 on v0

--- a/solution.py
+++ b/solution.py
@@ -3,6 +3,11 @@
 from jax import lax
 from jax.sharding import PartitionSpec as P
 from jax.experimental.layout import Layout, with_layout_constraint
+
+
+def gather_by_exchange(x, axis, dim):
+    copies = jnp.concatenate([x] * lax.axis_size(axis), axis=dim)
+    return lax.all_to_all(copies, axis, dim, dim, tiled=True)
 
 
 def slot_ranks(choices, experts):
@@ -17,7 +22,7 @@
     groups = lax.axis_size("dp")
     slots = hidden.shape[2] // experts
     width = w_down.shape[2]
-    w_whole = lax.all_gather(w_down, "dp", axis=1, tiled=True)[0]
+    w_whole = gather_by_exchange(w_down, "dp", 1)[0]
     out_slots = jnp.dot(hidden[0, 0], w_whole, preferred_element_type=jnp.float32).astype(
         jnp.bfloat16
     )

time: 197 us -> 418 us (2.12)
  local copies, waits for them, and re-layouts: 21.1 us -> 123 us
  waiting for transfers between devices: 44.9 us -> 109 us
  other arithmetic: 6.83 us -> 61.5 us
  starting transfers between devices: 24.4 us -> 19.2 us
    concatenate x0 -> x1, local copies, waits for them, and re-layouts: none -> 80.7 us  [gather_by_exchange(): copies = jnp.concatenate([x] * lax.axis_size(axis), axis=dim)]
    all_to_all x0 -> x1, waiting for transfers between devices: none -> 75.6 us  [gather_by_exchange(): return lax.all_to_all(copies, axis, dim, dim, tiled=True)]
    unnamed x1 -> x2, other arithmetic: 3.82 us -> 52.1 us
    unnamed x17 -> x21, local copies, waits for them, and re-layouts: 4.08 us -> 24.9 us
    all_to_all x1, starting transfers between devices: 20.3 us -> 9.92 us  [on_device(): lax.all_to_all(out_slots.reshape(experts, slots, width), 'expert', split_...]
    all_to_all x0 -> x1, starting transfers between devices: none -> 5.59 us  [gather_by_exchange(): return lax.all_to_all(copies, axis, dim, dim, tiled=True)]
    all_gather x1 -> x0, waiting for transfers between devices: 4.83 us -> none  [on_device(): w_whole = lax.all_gather(w_down, 'dp', axis=1, tiled=True)[0]]
    concatenate x0 -> x1, other arithmetic: none -> 4.78 us  [gather_by_exchange(): copies = jnp.concatenate([x] * lax.axis_size(axis), axis=dim)]
  transfers between devices with their start and end apart: 4 -> 4, of which waited for: 3 -> 2; matrix products, arithmetic and copies ran while one was open for 21% -> 46% of each run, Pallas kernels for 0% -> 0%
where the time goes in v1:
time: 418 us; the launch traced here: 417 us
  local copies, waits for them, and re-layouts  123 us (29%)
  waiting for transfers between devices  109 us (26%)
  blocking collectives  64.9 us (16%)
  other arithmetic  61.5 us (15%)
  matrix products  24.5 us (6%)
  starting transfers between devices  19.2 us (5%)
  between operations  14.2 us (3%)
    concatenate x1, local copies, waits for them, and re-layouts, gather_by_exchange(): copies = jnp.concatenate([x] * lax.axis_size(axis), axis=dim)  80.7 us
    all_to_all x1, waiting for transfers between devices, gather_by_exchange(): return lax.all_to_all(copies, axis, dim, dim, tiled=True)  75.6 us
    all_to_all x1, blocking collectives, on_device(): lax.all_to_all(outgoing.reshape(experts, 1, slots, width), 'expert', spli...  64.9 us
    unnamed x2, other arithmetic  52.1 us
    all_to_all x1, waiting for transfers between devices, on_device(): lax.all_to_all(out_slots.reshape(experts, slots, width), 'expert', split_...  33.7 us
    unnamed x21, local copies, waits for them, and re-layouts  24.9 us
    all_to_all x1, starting transfers between devices, on_device(): lax.all_to_all(out_slots.reshape(experts, slots, width), 'expert', split_...  9.92 us
    dot_general x1, matrix products, on_device(): jnp.einsum('rd,hd->rh', own_grads.reshape(-1, width), w_whole, preferred_...  8.63 us
  transfers between devices with their start and end apart: 4, of which 2 were waited for; matrix products, arithmetic and copies ran while one was open for 46% of the time, Pallas kernels for 0%

profile of v1, /device:TPU:1, one launch (start us, length us, event | category | flops | bytes accessed | tf_op | source)
XLA Modules:
  0.0 417.1 jit_solution(15471149811076187233)
XLA Ops:
  9.4 0.9 bitcast_convert_fusion.1
  11.1 2.5 scatter_custom_fusion
  13.7 1.6 reshape.99
  15.3 64.9 %all_to_all.30 = bf16[128,1,2,3584]{3,2,1,0:T(2,128)(2,1)S(1)} all-to-all(bf16[128,1,2,3584]{3,2,1,0:T(2,128)(2,1)} %reshape.99), channel_id=1, replica_groups=mesh['expert'=128,'dp'=4] {'expert'}, dimensions={0} | all-to-all | bytes 3670016 | tf_op jit(solution)/shard_map/all_to_all | solution.py:43
  80.2 1.4 copy.58
  81.7 4.8 %pad_maximum_fusion = bf16[1,1024,3584]{2,1,0:T(8,128)(2,1)S(1)} fusion(bf16[1,256,3584]{2,1,0:T(8,128)(2,1)} %param.6), kind=kLoop, calls=%fused_computation.2 | loop fusion | flops 29360128 | bytes 9175040 | tf_op jit(solution)/shard_map/concatenate | solution.py:9
  86.5 80.7 %copy.101 = bf16[1,1024,3584]{2,0,1:T(2,128)(2,1)} copy(bf16[1,1024,3584]{2,1,0:T(8,128)(2,1)S(1)} %pad_maximum_fusion) | data formatting | bytes 14680064 | tf_op jit(solution)/shard_map/concatenate | solution.py:9
  167.7 48.3 %reduce = bf16[1024,3584]{1,0:T(8,128)(2,1)} reduce(bf16[1024,1,3584]{2,1,0:T(2,128)(2,1)} %bitcast.81, bf16[]{:T(256)} %broadcast.58), dimensions={1}, to_apply=%bitcast.80.reduce_sub_computation | reduce | bytes 14680066
  215.9 9.0 %reshape.125 = bf16[4,2,458752]{2,1,0:T(2,128)(2,1)} reshape(bf16[1024,3584]{1,0:T(8,128)(2,1)} %reduce) | data formatting | bytes 14680064
  225.0 5.6 %all-to-all-start = ((bf16[4,2,458752]{2,1,0:T(2,128)(2,1)}), bf16[4,2,458752]{2,1,0:T(2,128)(2,1)}, u32[]{:S(2)}, u32[]{:S(2)}) async-start(bf16[4,2,458752]{2,1,0:T(2,128)(2,1)} %reshape.125), calls=%async_computation | async-start | bytes 14680064 | tf_op jit(solution)/shard_map/all_to_all | solution.py:10
  231.4 3.8 reduce.1
  236.2 75.6 %all-to-all-done = bf16[4,2,458752]{2,1,0:T(2,128)(2,1)} async-done(((bf16[4,2,458752]{2,1,0:T(2,128)(2,1)}), bf16[4,2,458752]{2,1,0:T(2,128)(2,1)}, u32[]{:S(2)}, u32[]{:S(2)}) %all-to-all-start) | async-done | bytes 7340064 | tf_op jit(solution)/shard_map/all_to_all | solution.py:10
  311.8 3.7 all-to-all-start.3
  315.5 11.4 %reshape.126 = bf16[1024,1,3584]{2,1,0:T(2,128)(2,1)} reshape(bf16[4,2,458752]{2,1,0:T(2,128)(2,1)} %all-to-all-done) | data formatting | bytes 14680064
  326.9 8.5 %fusion.15 = bf16[256,3584]{1,0:T(8,128)(2,1)} fusion(bf16[1,1024,3584]{2,0,1:T(2,128)(2,1)} %bitcast.82, bf16[1,1,256,1024]{3,2,1,0:T(8,128)(2,1)S(1)} %copy-done.1), kind=kOutput, calls=%fused_computation.12 | convolution fusion | flops 1879965696 | bytes 9699328 | tf_op jit(solution)/shard_map/dot_general | solution.py:26
  335.4 4.8 %reshape.96 = bf16[128,2,3584]{2,1,0:T(2,128)(2,1)} reshape(bf16[256,3584]{1,0:T(8,128)(2,1)} %fusion.15) | data formatting | bytes 3670016 | tf_op jit(solution)/shard_map/reshape | solution.py:30
  340.2 9.9 %all-to-all-start.1 = ((bf16[128,2,3584]{2,1,0:T(2,128)(2,1)}), bf16[128,2,3584]{2,1,0:T(2,128)(2,1)}, u32[]{:S(2)}, u32[]{:S(2)}) async-start(bf16[128,2,3584]{2,1,0:T(2,128)(2,1)} %reshape.96), calls=%async_computation.1 | async-start | bytes 3670016 | tf_op jit(solution)/shard_map/all_to_all | solution.py:29
  351.2 1.1 copy.61
  352.3 1.6 reshape_squeeze.6
  353.9 8.6 %fusion.27 = bf16[1,1,256,1024]{3,2,1,0:T(8,128)(2,1)} fusion(bf16[256,3584]{1,0:T(8,128)(2,1)} %reshape_squeeze.6, bf16[1,1024,3584]{2,0,1:T(2,128)(2,1)} %bitcast.83), kind=kOutput, calls=%fused_computation.19 | convolution fusion | flops 1879310336 | bytes 9699328 | tf_op jit(solution)/shard_map/rd,hd->rh/dot_general | solution.py:53
  362.6 33.7 %all-to-all-done.1 = bf16[128,2,3584]{2,1,0:T(2,128)(2,1)} async-done(((bf16[128,2,3584]{2,1,0:T(2,128)(2,1)}), bf16[128,2,3584]{2,1,0:T(2,128)(2,1)}, u32[]{:S(2)}, u32[]{:S(2)}) %all-to-all-start.1) | async-done | bytes 1835040 | tf_op jit(solution)/shard_map/all_to_all | solution.py:29
  396.3 4.1 reshape.97
  400.3 1.1 gather_fusion
  403.8 6.4 %fusion.18 = bf16[1,256,3584]{2,1,0:T(8,128)(2,1)} fusion(bf16[128,4,2,3584]{3,0,2,1:T(8,128)(2,1)} %all-gather.2.cloned.1.call-done, bf16[4,128,2,256]{3,0,2,1:T(4,128)(2,1)S(1)} %bitcast.87), kind=kOutput, calls=%fused_computation.13 | convolution fusion | flops 1879965696 | bytes 9699328 | tf_op jit(solution)/shard_map/gsch,sgcd->hd/dot_general | solution.py:58
  (43 shorter events, 8.7 us)
Async XLA Ops:
  7.2 396.6 %all-gather.2.cloned.1.call-start = ((), (), s32[]{:S(2)}) async-start(), calls=%async_computation.4 | async-start | bytes 9175040 | tf_op jit(solution)/shard_map/all_gather | solution.py:51
  225.0 5.6 %copy-start = (bf16[1,1,256,1024]{3,2,1,0:T(8,128)(2,1)S(1)}, bf16[1,1,256,1024]{3,2,1,0:T(8,128)(2,1)}, u32[]{:S(2)}) copy-start(bf16[1,1,256,1024]{3,2,1,0:T(8,128)(2,1)} %param.5) | copy-start | bytes 1572868
  225.0 86.8 %all-to-all-start = ((bf16[4,2,458752]{2,1,0:T(2,128)(2,1)}), bf16[4,2,458752]{2,1,0:T(2,128)(2,1)}, u32[]{:S(2)}, u32[]{:S(2)}) async-start(bf16[4,2,458752]{2,1,0:T(2,128)(2,1)} %reshape.125), calls=%async_computation | async-start | bytes 14680064 | tf_op jit(solution)/shard_map/all_to_all | solution.py:10
  311.8 28.4 %all-to-all-start.3 = ((bf16[4,2,32768]{2,1,0:T(2,128)(2,1)}), bf16[4,2,32768]{2,1,0:T(2,128)(2,1)S(1)}, u32[]{:S(2)}, u32[]{:S(2)}) async-start(bf16[4,2,32768]{2,1,0:T(2,128)(2,1)} %reshape.127), calls=%async_computation.3 | async-start | bytes 1048576 | tf_op jit(solution)/shard_map/all_to_all | solution.py:56
  315.5 11.4 %copy-start.1 = (bf16[1,1,256,1024]{3,2,1,0:T(8,128)(2,1)S(1)}, bf16[1,1,256,1024]{3,2,1,0:T(8,128)(2,1)}, u32[]{:S(2)}) copy-start(bf16[1,1,256,1024]{3,2,1,0:T(8,128)(2,1)} %param.5) | copy-start | bytes 1572868
  326.9 23.4 %copy-start.4 = (s32[1,16,8]{1,2,0:T(8,128)S(1)}, s32[1,16,8]{1,2,0:T(8,128)}, u32[]{:S(2)}) copy-start(s32[1,16,8]{1,2,0:T(8,128)} %param.7) | copy-start | bytes 1540
  326.9 23.6 %copy-start.5 = (f32[1,16,8]{1,2,0:T(8,128)S(1)}, f32[1,16,8]{1,2,0:T(8,128)}, u32[]{:S(2)}) copy-start(f32[1,16,8]{1,2,0:T(8,128)} %param.8) | copy-start | bytes 1540
  340.2 56.1 %all-to-all-start.1 = ((bf16[128,2,3584]{2,1,0:T(2,128)(2,1)}), bf16[128,2,3584]{2,1,0:T(2,128)(2,1)}, u32[]{:S(2)}, u32[]{:S(2)}) async-start(bf16[128,2,3584]{2,1,0:T(2,128)(2,1)} %reshape.96), calls=%async_computation.1 | async-start | bytes 3670016 | tf_op jit(solution)/shard_map/all_to_all | solution.py:29
  362.6 40.0 %copy-start.3 = (bf16[1,16,3584]{2,1,0:T(8,128)(2,1)S(1)}, bf16[1,16,3584]{2,1,0:T(8,128)(2,1)}, u32[]{:S(2)}) copy-start(bf16[1,16,3584]{2,1,0:T(8,128)(2,1)} %param.9) | copy-start | bytes 344068
  362.6 41.2 %copy-start.2 = (bf16[1,4,1,256,256]{4,1,3,2,0:T(4,128)(2,1)S(1)}, bf16[1,4,1,256,256]{4,1,3,2,0:T(4,128)(2,1)}, u32[]{:S(2)}) copy-start(bf16[1,4,1,256,256]{4,1,3,2,0:T(4,128)(2,1)} %copy.61) | copy-start | bytes 1572868
Sparse Core Ops, SparseCore 0:
  81.8 74.3 all-gather.1
